TPU v7x, 512 devices: a whole 4x4x16 slice. The times are simulated.
512 devices in a mesh: section: 8 (over y, x_hi), ctx: 16 (over z), dp: 4 (over x_lo, core).
Axes of the slice: x: 4 (x_hi: 2, x_lo: 2; x = x_hi * 2 + x_lo), y: 4, z: 16, core: 2. Of those that a mesh axis runs over, the one named last changes fastest.
Arguments:
- activations: bfloat16 [8, 4, 2048, 1280], P('section', 'dp', 'ctx'), may hold values from -6 to 6
- out_grads: bfloat16 [8, 4, 2048, 1280], P('section', 'dp', 'ctx'), may hold values from -6 to 6
- doc_ids: int32 [4, 16], replicated, may hold values from 0 to 3, never falling along the last dimension, each value on 1 to 12 neighbouring positions
- query_weight: bfloat16 [8, 1280, 640], P('section', None, 'dp'), may hold values from -0.195655948 to 0.195655948
- key_weight: bfloat16 [8, 1280, 640], P('section', None, 'dp'), may hold values from -3.0745935 to 3.0745935
- value_weight: bfloat16 [8, 1280, 640], P('section', None, 'dp'), may hold values from -0.15625 to 0.15625
- out_weight: bfloat16 [8, 640, 1280], P('section', 'dp'), may hold values from -0.25 to 0.25
Outputs:
- received_grad: bfloat16 [8, 4, 2048, 1280], P('section', 'dp', 'ctx')
Inputs may be any that keep to these rules, and one draw needn't show every extreme that they name: `doc_ids`: each page stack's documents are runs of whole blocks, numbered from 0 in order; a document covers at most 12 blocks.
All inputs are finite; a program needn't handle non-finite values.
Results may differ from a plain program's by a relative error of at most 0.0085.
The roundings to bfloat16 on the way count: a program that leaves them out, or rounds other values in their place, can miss the bound.
Values may be sent and summed in bfloat16 or wider, within the bound.
A program may use at most 128 MiB of HBM per device.

v0:
```python
import math
import jax
import jax.numpy as jnp
from jax import lax
from jax.sharding import PartitionSpec as P

HEAD_DIM = 80
BLOCK = 128
NEG = -1e30
HIGHEST = lax.Precision.HIGHEST


def from_behind(array, axis, by):
    length = lax.axis_size(axis)
    return lax.ppermute(array, axis, [(i, (i + by) % length) for i in range(length)])


def expand(allowed_blocks, query_len, key_len):
    page_count = allowed_blocks.shape[0]
    query_blocks = query_len // BLOCK
    key_blocks = key_len // BLOCK
    widened = jnp.broadcast_to(
        allowed_blocks[:, :, None, :, None], (page_count, query_blocks, BLOCK, key_blocks, BLOCK)
    )
    return widened.reshape(page_count, query_len, key_len)


def row_statistics(
    queries, out_grad, all_keys, all_values, block_table, my_offset, head_count, score_scale
):
    page_count, row_count, _ = queries.shape
    length = all_keys.shape[1]
    block_len = math.gcd(length, 512)
    query_four = queries.reshape(page_count, row_count, head_count, HEAD_DIM)
    grad_four = out_grad.reshape(page_count, row_count, head_count, HEAD_DIM)
    my_blocks = lax.dynamic_slice_in_dim(block_table, my_offset // BLOCK, row_count // BLOCK, 1)

    def row_visit(index, totals):
        key_offset = index * block_len
        key_block = lax.dynamic_slice_in_dim(all_keys, key_offset, block_len, 1).reshape(
            page_count, block_len, head_count, HEAD_DIM
        )
        value_block = lax.dynamic_slice_in_dim(all_values, key_offset, block_len, 1).reshape(
            page_count, block_len, head_count, HEAD_DIM
        )
        allowed = expand(
            lax.dynamic_slice_in_dim(my_blocks, key_offset // BLOCK, block_len // BLOCK, 2),
            row_count,
            block_len,
        )[:, None]
        old_max, old_sum, old_dot = totals
        scores = (
            jnp.einsum(
                "brhd,bkhd->bhrk",
                query_four,
                key_block,
                precision=HIGHEST,
                preferred_element_type=jnp.float32,
            )
            * score_scale
        )
        scores = jnp.where(allowed, scores, NEG)
        new_max = jnp.maximum(old_max, jnp.max(scores, axis=-1))
        weights = jnp.where(allowed, jnp.exp(scores - new_max[..., None]), 0.0)
        dprob = jnp.einsum(
            "brhd,bkhd->bhrk", grad_four, value_block, preferred_element_type=jnp.float32
        )
        factor = jnp.exp(old_max - new_max)
        return (
            new_max,
            old_sum * factor + jnp.sum(weights, axis=-1),
            old_dot * factor + jnp.sum(weights * dprob, axis=-1),
        )

    stat_shape = (page_count, head_count, row_count)
    zeros = jnp.zeros(stat_shape, jnp.float32)
    start_state = (jnp.full(stat_shape, NEG, jnp.float32), zeros, zeros)
    final_max, final_sum, final_dot = lax.fori_loop(0, length // block_len, row_visit, start_state)
    log_total = final_max + jnp.log(final_sum)
    row_delta = final_dot / final_sum
    return (jnp.transpose(log_total, (0, 2, 1)), jnp.transpose(row_delta, (0, 2, 1)))


def query_side(
    queries,
    out_grad,
    all_keys,
    all_values,
    block_table,
    my_offset,
    log_total,
    row_delta,
    head_count,
    score_scale,
):
    page_count, row_count, width = queries.shape
    length = all_keys.shape[1]
    block_len = math.gcd(length, 512)
    query_four = queries.reshape(page_count, row_count, head_count, HEAD_DIM)
    grad_four = out_grad.reshape(page_count, row_count, head_count, HEAD_DIM)
    log_heads = jnp.transpose(log_total, (0, 2, 1))
    delta_heads = jnp.transpose(row_delta, (0, 2, 1))
    my_blocks = lax.dynamic_slice_in_dim(block_table, my_offset // BLOCK, row_count // BLOCK, 1)

    def query_visit(index, totals):
        key_offset = index * block_len
        key_block = lax.dynamic_slice_in_dim(all_keys, key_offset, block_len, 1).reshape(
            page_count, block_len, head_count, HEAD_DIM
        )
        value_block = lax.dynamic_slice_in_dim(all_values, key_offset, block_len, 1).reshape(
            page_count, block_len, head_count, HEAD_DIM
        )
        allowed = expand(
            lax.dynamic_slice_in_dim(my_blocks, key_offset // BLOCK, block_len // BLOCK, 2),
            row_count,
            block_len,
        )[:, None]
        scores = (
            jnp.einsum(
                "brhd,bkhd->bhrk",
                query_four,
                key_block,
                precision=HIGHEST,
                preferred_element_type=jnp.float32,
            )
            * score_scale
        )
        scores = jnp.where(allowed, scores, NEG)
        prob = jnp.where(allowed, jnp.exp(scores - log_heads[..., None]), 0.0)
        dprob = jnp.einsum(
            "brhd,bkhd->bhrk", grad_four, value_block, preferred_element_type=jnp.float32
        )
        dscore = prob * (dprob - delta_heads[..., None])
        dscore_low = dscore.astype(jnp.bfloat16).astype(jnp.float32)
        return totals + jnp.einsum(
            "bhrk,bkhd->brhd",
            dscore_low,
            key_block,
            precision=HIGHEST,
            preferred_element_type=jnp.float32,
        )

    start_state = jnp.zeros((page_count, row_count, head_count, HEAD_DIM), jnp.float32)
    summed = lax.fori_loop(0, length // block_len, query_visit, start_state)
    return (summed * score_scale).astype(jnp.bfloat16).reshape(page_count, row_count, width)


def key_side(
    totals,
    portion,
    key_rows,
    value_rows,
    all_log_total,
    all_delta,
    block_table,
    my_offset,
    head_count,
    score_scale,
):
    part_queries, part_grads = portion
    page_count, part_len, _ = part_queries.shape
    row_count = key_rows.shape[1]
    block_len = math.gcd(part_len, 512)
    key_four = key_rows.reshape(page_count, row_count, head_count, HEAD_DIM)
    value_four = value_rows.reshape(page_count, row_count, head_count, HEAD_DIM)
    key_columns = lax.dynamic_slice_in_dim(block_table, my_offset // BLOCK, row_count // BLOCK, 2)

    def key_visit(index, state):
        query_offset = index * block_len
        query_part = lax.dynamic_slice_in_dim(part_queries, query_offset, block_len, 1).reshape(
            page_count, block_len, head_count, HEAD_DIM
        )
        grad_part = (
            lax.dynamic_slice_in_dim(part_grads, query_offset, block_len, 1)
            .astype(jnp.bfloat16)
            .reshape(page_count, block_len, head_count, HEAD_DIM)
        )
        log_part = jnp.transpose(
            lax.dynamic_slice_in_dim(all_log_total, query_offset, block_len, 1), (0, 2, 1)
        )
        delta_part = jnp.transpose(
            lax.dynamic_slice_in_dim(all_delta, query_offset, block_len, 1), (0, 2, 1)
        )
        allowed = expand(
            lax.dynamic_slice_in_dim(key_columns, query_offset // BLOCK, block_len // BLOCK, 1),
            block_len,
            row_count,
        )[:, None]
        key_total, value_total = state
        scores = (
            jnp.einsum(
                "bphd,brhd->bhpr",
                query_part,
                key_four,
                precision=HIGHEST,
                preferred_element_type=jnp.float32,
            )
            * score_scale
        )
        scores = jnp.where(allowed, scores, NEG)
        prob = jnp.where(allowed, jnp.exp(scores - log_part[..., None]), 0.0)
        value_total = value_total + jnp.einsum(
            "bhpr,bphd->brhd",
            prob.astype(jnp.bfloat16),
            grad_part,
            preferred_element_type=jnp.float32,
        )
        dprob = jnp.einsum(
            "bphd,brhd->bhpr", grad_part, value_four, preferred_element_type=jnp.float32
        )
        dscore = prob * (dprob - delta_part[..., None])
        dscore_low = dscore.astype(jnp.bfloat16).astype(jnp.float32)
        key_total = key_total + jnp.einsum(
            "bhpr,bphd->brhd",
            dscore_low,
            query_part,
            precision=HIGHEST,
            preferred_element_type=jnp.float32,
        )
        return (key_total, value_total)

    return lax.fori_loop(0, part_len // block_len, key_visit, totals)


def body(activations, out_grads, doc_ids, query_weight, key_weight, value_weight, out_weight):
    score_scale = HEAD_DIM ** (-0.5)
    row_count = activations.shape[2]
    my_offset = lax.axis_index("ctx") * row_count
    full_query, full_key, full_value, full_out = (
        lax.all_gather(query_weight, "dp", axis=2, tiled=True),
        lax.all_gather(key_weight, "dp", axis=2, tiled=True),
        lax.all_gather(value_weight, "dp", axis=2, tiled=True),
        lax.all_gather(out_weight, "dp", axis=1, tiled=True),
    )
    page_inputs = activations[0]
    page_upstream = out_grads[0]
    page_ids = lax.dynamic_slice_in_dim(doc_ids, lax.axis_index("dp"), 1, 0)
    proj_query = full_query[0]
    proj_key = full_key[0]
    proj_value = full_value[0]
    proj_out = full_out[0]
    head_count = proj_query.shape[1] // HEAD_DIM
    inputs = page_inputs.astype(jnp.float32)
    inv_rms = lax.rsqrt(jnp.mean(inputs * inputs, axis=-1, keepdims=True) + 1e-05)
    normed = (inputs * inv_rms).astype(jnp.bfloat16)
    queries = jnp.einsum("brd,dh->brh", normed, proj_query, preferred_element_type=jnp.float32)
    key_rows = jnp.einsum("brd,dh->brh", normed, proj_key, preferred_element_type=jnp.float32)
    value_rows = jnp.einsum(
        "brd,dh->brh", normed, proj_value, preferred_element_type=jnp.float32
    ).astype(jnp.bfloat16)
    out_grad = jnp.einsum(
        "brd,hd->brh", page_upstream, proj_out, preferred_element_type=jnp.float32
    ).astype(jnp.bfloat16)
    block_table = page_ids[:, :, None] == page_ids[:, None, :]
    all_keys, wide_values = (
        lax.all_gather(key_rows, "ctx", axis=1, tiled=True),
        lax.all_gather(value_rows.astype(jnp.float32), "ctx", axis=1, tiled=True),
    )
    all_values = wide_values.astype(jnp.bfloat16)
    log_total, row_delta = row_statistics(
        queries, out_grad, all_keys, all_values, block_table, my_offset, head_count, score_scale
    )
    all_log_total, all_delta = (
        lax.all_gather(log_total, "ctx", axis=1, tiled=True),
        lax.all_gather(row_delta, "ctx", axis=1, tiled=True),
    )
    q_grad = query_side(
        queries,
        out_grad,
        all_keys,
        all_values,
        block_table,
        my_offset,
        log_total,
        row_delta,
        head_count,
        score_scale,
    )
    empty = jnp.zeros((key_rows.shape[0], row_count, head_count, HEAD_DIM), jnp.float32)
    key_total, value_total = key_side(
        (empty, empty),
        (
            lax.all_gather(queries, "ctx", axis=1, tiled=True),
            lax.all_gather(out_grad.astype(jnp.float32), "ctx", axis=1, tiled=True),
        ),
        key_rows,
        value_rows,
        all_log_total,
        all_delta,
        block_table,
        my_offset,
        head_count,
        score_scale,
    )
    k_grad = (key_total * score_scale).astype(jnp.bfloat16).reshape(key_rows.shape)
    v_grad = value_total.astype(jnp.bfloat16).reshape(value_rows.shape)
    summed = jnp.einsum("brh,dh->brd", q_grad, proj_query, preferred_element_type=jnp.float32)
    summed = summed + jnp.einsum(
        "brh,dh->brd", k_grad, proj_key, preferred_element_type=jnp.float32
    )
    normed_grad = summed + jnp.einsum(
        "brh,dh->brd", v_grad, proj_value, preferred_element_type=jnp.float32
    )
    branch = inv_rms * normed_grad - inputs * inv_rms**3 * jnp.mean(
        normed_grad * inputs, axis=-1, keepdims=True
    )
    branch_grad = branch.astype(jnp.bfloat16)[None]
    return from_behind(branch_grad, "section", -1)


def solution(mesh):
    return jax.shard_map(
        body,
        mesh=mesh,
        in_specs=(
            P("section", "dp", "ctx", None),
            P("section", "dp", "ctx", None),
            P(),
            P("section", None, "dp"),
            P("section", None, "dp"),
            P("section", None, "dp"),
            P("section", "dp", None),
        ),
        out_specs=P("section", "dp", "ctx", None),
        check_vma=False,
    )
```

profile of v0, /device:TPU:62, one launch (start us, length us, event | category | flops | bytes accessed | tf_op | source)
XLA Modules:
  0.0 580.7 jit_solution(2038924234252000097)
XLA Ops:
  10.5 35.1 %all-gather.17.cloned.1.call-done = bf16[1,1280,640]{1,2,0:T(8,128)(2,1)} async-done(((bf16[1,1280,160]{1,2,0:T(8,128)(2,1)}), bf16[1,1280,640]{1,2,0:T(8,128)(2,1)}) %all-gather.17.cloned.1.call-update) | async-done | bytes 1638416 | tf_op jit(solution)/shard_map/all_gather | solution.py:232
  48.4 33.3 %all-gather.13.cloned.1.call-done = bf16[1,1280,640]{1,2,0:T(8,128)(2,1)} async-done(((bf16[1,1280,160]{1,2,0:T(8,128)(2,1)}), bf16[1,1280,640]{1,2,0:T(8,128)(2,1)}) %all-gather.13.cloned.1.call-update) | async-done | bytes 1638416 | tf_op jit(solution)/shard_map/all_gather | solution.py:231
  84.6 33.3 %all-gather.19.cloned.1.call-done = bf16[1,640,1280]{2,1,0:T(8,128)(2,1)} async-done(((bf16[1,160,1280]{2,1,0:T(8,128)(2,1)}), bf16[1,640,1280]{2,1,0:T(8,128)(2,1)}) %all-gather.19.cloned.1.call-update) | async-done | bytes 1638416 | tf_op jit(solution)/shard_map/all_gather | solution.py:233
  124.9 28.9 %all-gather.15.cloned.1.call-done = bf16[1,1280,640]{1,2,0:T(8,128)(2,1)} async-done(((bf16[1,1280,160]{1,2,0:T(8,128)(2,1)}), bf16[1,1280,640]{1,2,0:T(8,128)(2,1)}) %all-gather.15.cloned.1.call-update) | async-done | bytes 1638416 | tf_op jit(solution)/shard_map/all_gather | solution.py:230
  158.1 74.2 %all-gather.23.cloned.1.call-done = bf16[2048,640]{1,0:T(8,128)(2,1)} async-done(((bf16[128,640]{1,0:T(8,128)(2,1)}), bf16[2048,640]{1,0:T(8,128)(2,1)}) %all-gather.23.cloned.1.call-update) | async-done | bytes 2621456 | tf_op jit(solution)/shard_map/all_gather | solution.py:257
  232.4 4.5 copy.22
  236.8 74.7 %all-gather.21.cloned.1.call-done = f32[2048,640]{1,0:T(8,128)} async-done(((f32[128,640]{1,0:T(8,128)}), f32[2048,640]{1,0:T(8,128)}) %all-gather.21.cloned.1.call-update) | async-done | bytes 5242896 | tf_op jit(solution)/shard_map/all_gather | solution.py:256
  311.6 6.0 %copy.23 = f32[1,2048,640]{1,2,0:T(8,128)} copy(f32[1,2048,640]{2,1,0:T(8,128)} %bitcast.272) | data formatting | bytes 10485760
  317.6 42.2 %while.54 = (s32[]{:T(128)}, f32[1,8,128]{2,1,0:T(8,128)S(1)}, f32[1,8,128]{2,1,0:T(8,128)S(1)}, f32[1,8,128]{2,1,0:T(8,128)S(1)}, pred[1,1,16]{2,1,0:T(4,128)(4...) while((s32[]{:T(128)}, f32[1,8,128]{2,1,0:T(8,128)S(1)}, ...), condition=%wide.region_5.6_spmd.clone, body=%wide.region_1.5_spmd.clone.sunk | while | flops 594549760 | bytes 12757413 | solution.py:78
  332.3 3.6 bitcast_reduce_fusion.2
  353.4 3.6 bitcast_reduce_fusion.2
  359.8 29.6 %all_gather.37 = f32[1,2048,8]{1,2,0:T(8,128)} all-gather(f32[1,128,8]{1,2,0:T(8,128)S(1)} %bitcast.287), channel_id=1, replica_groups=mesh['section'=8,'ctx'=16,'dp'=4] {'ctx'}, dimensions={1}, use_global_device_ids=true | all-gather | bytes 69632 | tf_op jit(solution)/shard_map/all_gather | solution.py:264
  389.4 30.9 %all_gather.39 = f32[1,2048,8]{1,2,0:T(8,128)} all-gather(f32[1,128,8]{1,2,0:T(8,128)S(1)} %bitcast.285), channel_id=1, replica_groups=mesh['section'=8,'ctx'=16,'dp'=4] {'ctx'}, dimensions={1}, use_global_device_ids=true | all-gather | bytes 69632 | tf_op jit(solution)/shard_map/all_gather | solution.py:265
  420.3 56.8 %while.55 = (s32[]{:T(128)}, f32[1,128,8,80]{1,3,2,0:T(8,128)}, f32[1,2048,640]{1,2,0:T(8,128)}, pred[1,1,16]{2,1,0:T(4,128)(4,1)}, f32[1,128,8,80]{3,2,1,0:T(8,...) while((s32[]{:T(128)}, f32[1,128,8,80]{1,3,2,0:T(8,128)}, ...), condition=%wide.region_7.8_spmd.clone, body=%wide.region_6.7_spmd.clone.sunk | while | flops 1094352896 | bytes 14656932 | solution.py:144
  421.7 4.8 fusion.99
  435.2 4.8 fusion.99
  449.6 4.8 fusion.99
  464.1 4.8 fusion.99
  478.7 76.3 %while.56 = (s32[]{:T(128)}, f32[1,128,8,80]{1,3,2,0:T(8,128)S(1)}, f32[1,128,8,80]{1,3,2,0:T(8,128)}, f32[1,2048,640]{2,1,0:T(8,128)}, pred[1,16,1]{1,2,0:T(4,1...) while((s32[]{:T(128)}, f32[1,128,8,80]{1,3,2,0:T(8,128)S(1)}, ...), condition=%wide.region_9.10_spmd.clone, body=%wide.region_8.9_spmd.clone.sunk | while | flops 1178927104 | bytes 26019420 | solution.py:222
  482.6 5.4 exponential_select_fusion.2
  501.6 5.4 exponential_select_fusion.2
  520.7 5.4 exponential_select_fusion.2
  539.8 5.4 exponential_select_fusion.2
  563.7 9.3 %collective-permute-done = bf16[1,1,128,1280]{3,2,1,0:T(8,128)(2,1)S(1)} collective-permute-done((bf16[1,1,128,1280]{3,2,1,0:T(8,128)(2,1)S(1)}, bf16[1,1,128,1280]{3,2,1,0:T(8,128)(2,1)S(1)}, u32[]{:S(2)}, u32[]{:S(2)}) %collective-permute-start) | collective-permute-done | bytes 327712 | tf_op jit(solution)/shard_map/ppermute | solution.py:15
  (205 shorter events, 158.6 us)
Async XLA Ops:
  6.5 111.3 %copy-start = (bf16[1,1,128,1280]{3,2,1,0:T(8,128)(2,1)S(1)}, bf16[1,1,128,1280]{3,2,1,0:T(8,128)(2,1)}, u32[]{:S(2)}) copy-start(bf16[1,1,128,1280]{3,2,1,0:T(8,128)(2,1)} %param.14) | copy-start | bytes 983044
  6.5 39.0 %copy-start.2 = (bf16[1,1,128,1280]{3,2,1,0:T(8,128)(2,1)S(1)}, bf16[1,1,128,1280]{3,2,1,0:T(8,128)(2,1)}, u32[]{:S(2)}) copy-start(bf16[1,1,128,1280]{3,2,1,0:T(8,128)(2,1)} %param.13) | copy-start | bytes 983044
  6.5 39.0 %all-gather.17.cloned.1.call-start = ((), (), s32[]{:S(2)}) async-start(), calls=%async_computation.2 | async-start | bytes 2048000 | tf_op jit(solution)/shard_map/all_gather | solution.py:232
  7.3 74.4 %all-gather.13.cloned.1.call-start = ((), (), s32[]{:S(2)}) async-start(), calls=%async_computation | async-start | bytes 2048000 | tf_op jit(solution)/shard_map/all_gather | solution.py:231
  8.0 109.8 %all-gather.19.cloned.1.call-start = ((), (), s32[]{:S(2)}) async-start(), calls=%async_computation.3 | async-start | bytes 2048000 | tf_op jit(solution)/shard_map/all_gather | solution.py:233
  8.7 145.1 %all-gather.15.cloned.1.call-start = ((), (), s32[]{:S(2)}) async-start(), calls=%async_computation.1 | async-start | bytes 2048000 | tf_op jit(solution)/shard_map/all_gather | solution.py:230
  9.3 223.0 %all-gather.23.cloned.1.call-start = ((), (), s32[]{:S(2)}) async-start(), calls=%async_computation.5 | async-start | bytes 2785280 | tf_op jit(solution)/shard_map/all_gather | solution.py:257
  48.3 263.2 %all-gather.21.cloned.1.call-start = ((), (), s32[]{:S(2)}) async-start(), calls=%async_computation.4 | async-start | bytes 5570560 | tf_op jit(solution)/shard_map/all_gather | solution.py:256
  84.5 39.3 %copy-start.9 = (f32[128,640]{1,0:T(8,128)S(1)}, f32[128,640]{1,0:T(8,128)}, u32[]{:S(2)}) copy-start(f32[128,640]{1,0:T(8,128)} %fusion.26) | copy-start | bytes 983044
  84.5 40.2 %copy-start.10 = (bf16[128,640]{1,0:T(8,128)(2,1)S(1)}, bf16[128,640]{1,0:T(8,128)(2,1)}, u32[]{:S(2)}) copy-start(bf16[128,640]{1,0:T(8,128)(2,1)} %fusion.28) | copy-start | bytes 491524
  84.5 394.2 %all-gather.27.cloned.1.call-start = ((), (), s32[]{:S(2)}) async-start(), calls=%async_computation.7 | async-start | bytes 2785280 | tf_op jit(solution)/shard_map/all_gather | solution.py:284
  120.6 358.1 %all-gather.25.cloned.1.call-start = ((), (), s32[]{:S(2)}) async-start(), calls=%async_computation.6 | async-start | bytes 5570560 | tf_op jit(solution)/shard_map/all_gather | solution.py:283
  420.3 58.4 %copy-start.1 = (f32[1,128,8,80]{1,3,2,0:T(8,128)S(1)}, f32[1,128,8,80]{1,3,2,0:T(8,128)}, u32[]{:S(2)}) copy-start(f32[1,128,8,80]{1,3,2,0:T(8,128)} %custom-call.4) | copy-start | bytes 983044
  478.7 3.7 copy-start.12
  478.7 3.8 copy-start.11
  494.2 2.5 copy-start.4
  497.8 3.7 copy-start.12
  497.8 3.8 copy-start.11
  516.9 3.7 copy-start.12
  516.9 3.8 copy-start.11
  536.0 3.7 copy-start.12
  536.0 3.8 copy-start.11
  555.0 3.2 copy-start.7
  560.5 12.6 %collective-permute-start = (bf16[1,1,128,1280]{3,2,1,0:T(8,128)(2,1)S(1)}, bf16[1,1,128,1280]{3,2,1,0:T(8,128)(2,1)S(1)}, u32[]{:S(2)}, u32[]{:S(2)}) collective-permute-start(bf16[1,1,128,1280]{3,2,1,0:T(8,128)(2,1)S(1)} %fusion.44), channel_id=1, source_target_pairs={{0,448},{64,0},{128,64},{192,128},{256,192},{320,256},{384,320},{4... | collective-permute-start | bytes 983048 | tf_op jit(solution)/shard_map/ppermute | solution.py:15
  (10 other events, 14.3 us)
Sparse Core Ops, SparseCore 0:
  9.5 36.0 all-gather.16
  47.7 33.9 all-gather.12
  83.8 33.9 all-gather.18
  119.8 33.9 all-gather.14
  155.7 76.5 all-gather.22
  234.3 77.2 all-gather.20
  313.6 71.2 all-gather.26
  387.0 77.6 all-gather.24
where the time goes:
time: 583 us; the launch traced here: 581 us
  waiting for transfers between devices  292 us (50%)
  matrix products  120 us (21%)
  local copies, waits for them, and re-layouts  83.9 us (14%)
  blocking collectives  60.5 us (10%)
  between operations  13.7 us (2%)
  other arithmetic  6.74 us (1%)
    all_gather x1, waiting for transfers between devices, body(): lax.all_gather(key_rows, 'ctx', axis=1, tiled=True)  74.7 us
    all_gather x1, waiting for transfers between devices, body(): lax.all_gather(value_rows.astype(jnp.float32), 'ctx', axis=1, tiled=True)  74.2 us
    all_gather x1, waiting for transfers between devices, body(): lax.all_gather(value_weight, 'dp', axis=2, tiled=True)  35.1 us
    all_gather x1, waiting for transfers between devices, body(): lax.all_gather(key_weight, 'dp', axis=2, tiled=True)  33.3 us
    all_gather x1, waiting for transfers between devices, body(): lax.all_gather(out_weight, 'dp', axis=1, tiled=True)  33.3 us
    all_gather x1, blocking collectives, body(): lax.all_gather(row_delta, 'ctx', axis=1, tiled=True)  30.9 us
    all_gather x1, blocking collectives, body(): lax.all_gather(log_total, 'ctx', axis=1, tiled=True)  29.6 us
    all_gather x1, waiting for transfers between devices, body(): lax.all_gather(query_weight, 'dp', axis=2, tiled=True)  28.9 us
  transfers between devices with their start and end apart: 9, of which 7 were waited for; matrix products, arithmetic and copies ran while one was open for 22% of the time, Pallas kernels for 0%

commit v1 on v0

--- a/solution.py
+++ b/solution.py
@@ -8,6 +8,12 @@
 BLOCK = 128
 NEG = -1e30
 HIGHEST = lax.Precision.HIGHEST
+
+
+def _prepare_pipes(a0):
+    b_next = jax.lax.all_to_all(jnp.stack(jax.lax.axis_size("ctx") * [a0], 0), "ctx", 0, 0)
+    y2 = jnp.concatenate(b_next, 1)
+    return y2
 
 
 def from_behind(array, axis, by):
@@ -262,7 +268,7 @@
     )
     all_log_total, all_delta = (
         lax.all_gather(log_total, "ctx", axis=1, tiled=True),
-        lax.all_gather(row_delta, "ctx", axis=1, tiled=True),
+        _prepare_pipes(row_delta),
     )
     q_grad = query_side(
         queries,

time: 583 us -> 569 us (0.976)
  the two profiles are of different devices: /device:TPU:62 before, /device:TPU:28 now
where the time goes in v1:
time: 569 us; the launch traced here: 566 us
  waiting for transfers between devices  309 us (54%)
  matrix products  124 us (22%)
  local copies, waits for them, and re-layouts  72.5 us (13%)
  blocking collectives  30.2 us (5%)
  between operations  13.7 us (2%)
  starting transfers between devices  9.5 us (2%)
  other arithmetic  6.72 us (1%)
    all_gather x1, waiting for transfers between devices, body(): lax.all_gather(value_rows.astype(jnp.float32), 'ctx', axis=1, tiled=True)  75.4 us
    all_gather x1, waiting for transfers between devices, body(): lax.all_gather(key_rows, 'ctx', axis=1, tiled=True)  74.9 us
    all_gather x1, waiting for transfers between devices, body(): lax.all_gather(value_weight, 'dp', axis=2, tiled=True)  35.2 us
    all_gather x1, waiting for transfers between devices, body(): lax.all_gather(key_weight, 'dp', axis=2, tiled=True)  33.3 us
    all_gather x1, waiting for transfers between devices, body(): lax.all_gather(out_weight, 'dp', axis=1, tiled=True)  33.2 us
    all_gather x1, blocking collectives, body(): lax.all_gather(log_total, 'ctx', axis=1, tiled=True)  30.2 us
    all_gather x1, waiting for transfers between devices, body(): lax.all_gather(query_weight, 'dp', axis=2, tiled=True)  28.2 us
    dot_general x4, matrix products, key_visit(): jnp.einsum('bphd,brhd->bhpr', query_part, key_four, precision=HIGHEST, pr...  21.8 us
  transfers between devices with their start and end apart: 10, of which 8 were waited for; matrix products, arithmetic and copies ran while one was open for 21% of the time, Pallas kernels for 0%

profile of v1, /device:TPU:28, one launch (start us, length us, event | category | flops | bytes accessed | tf_op | source)
XLA Modules:
  0.0 566.5 jit_solution(12936515090894765828)
XLA Ops:
  11.1 35.2 %all-gather.17.cloned.1.call-done = bf16[1,1280,640]{1,2,0:T(8,128)(2,1)} async-done(((bf16[1,1280,160]{1,2,0:T(8,128)(2,1)}), bf16[1,1280,640]{1,2,0:T(8,128)(2,1)}) %all-gather.17.cloned.1.call-update) | async-done | bytes 1638416 | tf_op jit(solution)/shard_map/all_gather | solution.py:238
  49.1 33.3 %all-gather.13.cloned.1.call-done = bf16[1,1280,640]{1,2,0:T(8,128)(2,1)} async-done(((bf16[1,1280,160]{1,2,0:T(8,128)(2,1)}), bf16[1,1280,640]{1,2,0:T(8,128)(2,1)}) %all-gather.13.cloned.1.call-update) | async-done | bytes 1638416 | tf_op jit(solution)/shard_map/all_gather | solution.py:237
  85.3 33.2 %all-gather.19.cloned.1.call-done = bf16[1,640,1280]{2,1,0:T(8,128)(2,1)} async-done(((bf16[1,160,1280]{2,1,0:T(8,128)(2,1)}), bf16[1,640,1280]{2,1,0:T(8,128)(2,1)}) %all-gather.19.cloned.1.call-update) | async-done | bytes 1638416 | tf_op jit(solution)/shard_map/all_gather | solution.py:239
  126.3 28.2 %all-gather.15.cloned.1.call-done = bf16[1,1280,640]{1,2,0:T(8,128)(2,1)} async-done(((bf16[1,1280,160]{1,2,0:T(8,128)(2,1)}), bf16[1,1280,640]{1,2,0:T(8,128)(2,1)}) %all-gather.15.cloned.1.call-update) | async-done | bytes 1638416 | tf_op jit(solution)/shard_map/all_gather | solution.py:236
  157.4 75.4 %all-gather.23.cloned.1.call-done = bf16[2048,640]{1,0:T(8,128)(2,1)} async-done(((bf16[128,640]{1,0:T(8,128)(2,1)}), bf16[2048,640]{1,0:T(8,128)(2,1)}) %all-gather.23.cloned.1.call-update) | async-done | bytes 2621456 | tf_op jit(solution)/shard_map/all_gather | solution.py:263
  232.8 4.5 copy.37
  237.2 74.9 %all-gather.21.cloned.1.call-done = f32[2048,640]{1,0:T(8,128)} async-done(((f32[128,640]{1,0:T(8,128)}), f32[2048,640]{1,0:T(8,128)}) %all-gather.21.cloned.1.call-update) | async-done | bytes 5242896 | tf_op jit(solution)/shard_map/all_gather | solution.py:262
  312.2 6.0 %copy.38 = f32[1,2048,640]{1,2,0:T(8,128)} copy(f32[1,2048,640]{2,1,0:T(8,128)} %bitcast.279) | data formatting | bytes 10485760
  318.2 35.6 %while.54 = (s32[]{:T(128)}, f32[1,8,128]{2,1,0:T(8,128)S(1)}, f32[1,8,128]{2,1,0:T(8,128)S(1)}, f32[1,8,128]{2,1,0:T(8,128)S(1)}, pred[1,1,16]{2,1,0:T(4,128)(4...) while((s32[]{:T(128)}, f32[1,8,128]{2,1,0:T(8,128)S(1)}, ...), condition=%wide.region_5.6_spmd.clone, body=%wide.region_1.5_spmd.clone.sunk | while | flops 594549760 | bytes 12757413 | solution.py:84
  320.9 3.6 bitcast_reduce_fusion.2
  354.4 6.8 %all-to-all-start = ((f32[16,1,128,8]{2,3,1,0:T(8,128)}), f32[16,1,128,8]{2,3,1,0:T(8,128)S(1)}, u32[]{:S(2)}, u32[]{:S(2)}) async-start(f32[16,1,128,8]{2,3,1,0:T(8,128)} %stack.2), calls=%async_computation | async-start | bytes 131072 | tf_op jit(solution)/shard_map/all_to_all | solution.py:14
  361.2 30.2 %all_gather.34 = f32[1,2048,8]{1,2,0:T(8,128)S(1)} all-gather(f32[1,128,8]{1,2,0:T(8,128)S(1)} %bitcast.291), channel_id=1, replica_groups=mesh['section'=8,'ctx'=16,'dp'=4] {'ctx'}, dimensions={1}, use_global_device_ids=true | all-gather | bytes 69632 | tf_op jit(solution)/shard_map/all_gather | solution.py:270
  391.4 55.9 %while.55 = (s32[]{:T(128)}, f32[1,128,8,80]{1,3,2,0:T(8,128)}, f32[1,2048,640]{1,2,0:T(8,128)}, pred[1,1,16]{2,1,0:T(4,128)(4,1)}, f32[1,128,8,80]{1,3,2,0:T(8,...) while((s32[]{:T(128)}, f32[1,128,8,80]{1,3,2,0:T(8,128)}, ...), condition=%wide.region_7.8_spmd.clone, body=%wide.region_6.7_spmd.clone.sunk | while | flops 1094352896 | bytes 17933908 | solution.py:150
  392.8 4.8 fusion.99
  406.8 4.8 fusion.99
  420.8 4.8 fusion.99
  434.8 4.8 fusion.99
  451.1 15.7 %all-gather.25.cloned.1.call-done = f32[2048,640]{1,0:T(8,128)} async-done(((f32[128,640]{1,0:T(8,128)}), f32[2048,640]{1,0:T(8,128)}) %all-gather.25.cloned.1.call-update) | async-done | bytes 5242896 | tf_op jit(solution)/shard_map/all_gather | solution.py:289
  466.9 75.3 %while.56 = (s32[]{:T(128)}, f32[1,128,8,80]{1,3,2,0:T(8,128)S(1)}, f32[1,128,8,80]{1,3,2,0:T(8,128)}, f32[1,2048,640]{2,1,0:T(8,128)}, pred[1,16,1]{1,2,0:T(4,1...) while((s32[]{:T(128)}, f32[1,128,8,80]{1,3,2,0:T(8,128)S(1)}, ...), condition=%wide.region_9.10_spmd.clone, body=%wide.region_8.9_spmd.clone.sunk | while | flops 1178927104 | bytes 24708584 | solution.py:228
  470.5 5.4 exponential_select_fusion.2
  489.3 5.4 exponential_select_fusion.2
  508.1 5.4 exponential_select_fusion.2
  527.0 5.4 exponential_select_fusion.2
  548.8 10.2 %collective-permute-done = bf16[1,1,128,1280]{3,2,1,0:T(8,128)(2,1)S(1)} collective-permute-done((bf16[1,1,128,1280]{3,2,1,0:T(8,128)(2,1)S(1)}, bf16[1,1,128,1280]{3,2,1,0:T(8,128)(2,1)S(1)}, u32[]{:S(2)}, u32[]{:S(2)}) %collective-permute-start) | collective-permute-done | bytes 327712 | tf_op jit(solution)/shard_map/ppermute | solution.py:21
  (226 shorter events, 153.6 us)
Async XLA Ops:
  6.5 112.0 %copy-start = (bf16[1,1,128,1280]{3,2,1,0:T(8,128)(2,1)S(1)}, bf16[1,1,128,1280]{3,2,1,0:T(8,128)(2,1)}, u32[]{:S(2)}) copy-start(bf16[1,1,128,1280]{3,2,1,0:T(8,128)(2,1)} %param.14) | copy-start | bytes 983044
  6.5 39.8 %copy-start.4 = (bf16[1,1,128,1280]{3,2,1,0:T(8,128)(2,1)S(1)}, bf16[1,1,128,1280]{3,2,1,0:T(8,128)(2,1)}, u32[]{:S(2)}) copy-start(bf16[1,1,128,1280]{3,2,1,0:T(8,128)(2,1)} %param.13) | copy-start | bytes 983044
  6.5 39.7 %all-gather.17.cloned.1.call-start = ((), (), s32[]{:S(2)}) async-start(), calls=%async_computation.3 | async-start | bytes 2048000 | tf_op jit(solution)/shard_map/all_gather | solution.py:238
  7.3 75.1 %all-gather.13.cloned.1.call-start = ((), (), s32[]{:S(2)}) async-start(), calls=%async_computation.1 | async-start | bytes 2048000 | tf_op jit(solution)/shard_map/all_gather | solution.py:237
  8.0 110.5 %all-gather.19.cloned.1.call-start = ((), (), s32[]{:S(2)}) async-start(), calls=%async_computation.4 | async-start | bytes 2048000 | tf_op jit(solution)/shard_map/all_gather | solution.py:239
  8.7 145.8 %all-gather.15.cloned.1.call-start = ((), (), s32[]{:S(2)}) async-start(), calls=%async_computation.2 | async-start | bytes 2048000 | tf_op jit(solution)/shard_map/all_gather | solution.py:236
  9.3 223.5 %all-gather.23.cloned.1.call-start = ((), (), s32[]{:S(2)}) async-start(), calls=%async_computation.6 | async-start | bytes 2785280 | tf_op jit(solution)/shard_map/all_gather | solution.py:263
  11.1 143.4 %copy-start.13 = (f32[128]{0:T(128)}, f32[128]{0:T(128)S(1)}, u32[]{:S(2)}) copy-start(f32[128]{0:T(128)S(1)} %get-tuple-element.941) | copy-start | bytes 1540
  49.1 263.1 %all-gather.21.cloned.1.call-start = ((), (), s32[]{:S(2)}) async-start(), calls=%async_computation.5 | async-start | bytes 5570560 | tf_op jit(solution)/shard_map/all_gather | solution.py:262
  85.2 39.4 %copy-start.10 = (f32[128,640]{1,0:T(8,128)S(1)}, f32[128,640]{1,0:T(8,128)}, u32[]{:S(2)}) copy-start(f32[128,640]{1,0:T(8,128)} %fusion.26) | copy-start | bytes 983044
  85.2 40.2 %copy-start.11 = (bf16[128,640]{1,0:T(8,128)(2,1)S(1)}, bf16[128,640]{1,0:T(8,128)(2,1)}, u32[]{:S(2)}) copy-start(bf16[128,640]{1,0:T(8,128)(2,1)} %fusion.28) | copy-start | bytes 491524
  85.2 365.9 %all-gather.27.cloned.1.call-start = ((), (), s32[]{:S(2)}) async-start(), calls=%async_computation.8 | async-start | bytes 2785280 | tf_op jit(solution)/shard_map/all_gather | solution.py:290
  121.3 345.6 %all-gather.25.cloned.1.call-start = ((), (), s32[]{:S(2)}) async-start(), calls=%async_computation.7 | async-start | bytes 5570560 | tf_op jit(solution)/shard_map/all_gather | solution.py:289
  354.4 112.5 %all-to-all-start = ((f32[16,1,128,8]{2,3,1,0:T(8,128)}), f32[16,1,128,8]{2,3,1,0:T(8,128)S(1)}, u32[]{:S(2)}, u32[]{:S(2)}) async-start(f32[16,1,128,8]{2,3,1,0:T(8,128)} %stack.2), calls=%async_computation | async-start | bytes 131072 | tf_op jit(solution)/shard_map/all_to_all | solution.py:14
  392.8 6.0 %copy-start.17 = (pred[1,1,16]{2,1,0:T(4,128)(4,1)S(1)}, pred[1,1,16]{2,1,0:T(4,128)(4,1)}, u32[]{:S(2)}) copy-start(pred[1,1,16]{2,1,0:T(4,128)(4,1)} %get-tuple-element.1215) | copy-start | bytes 52 | tf_op jit(solution)/shard_map/while
  392.8 6.1 %copy-start.12 = (bf16[1,128,8,80]{1,3,2,0:T(8,128)(2,1)S(1)}, bf16[1,128,8,80]{1,3,2,0:T(8,128)(2,1)}, u32[]{:S(2)}) copy-start(bf16[1,128,8,80]{1,3,2,0:T(8,128)(2,1)} %get-tuple-element.1219) | copy-start | bytes 491524 | tf_op jit(solution)/shard_map/while
  406.8 6.0 %copy-start.17 = (pred[1,1,16]{2,1,0:T(4,128)(4,1)S(1)}, pred[1,1,16]{2,1,0:T(4,128)(4,1)}, u32[]{:S(2)}) copy-start(pred[1,1,16]{2,1,0:T(4,128)(4,1)} %get-tuple-element.1215) | copy-start | bytes 52 | tf_op jit(solution)/shard_map/while
  406.8 6.1 %copy-start.12 = (bf16[1,128,8,80]{1,3,2,0:T(8,128)(2,1)S(1)}, bf16[1,128,8,80]{1,3,2,0:T(8,128)(2,1)}, u32[]{:S(2)}) copy-start(bf16[1,128,8,80]{1,3,2,0:T(8,128)(2,1)} %get-tuple-element.1219) | copy-start | bytes 491524 | tf_op jit(solution)/shard_map/while
  420.7 6.0 %copy-start.17 = (pred[1,1,16]{2,1,0:T(4,128)(4,1)S(1)}, pred[1,1,16]{2,1,0:T(4,128)(4,1)}, u32[]{:S(2)}) copy-start(pred[1,1,16]{2,1,0:T(4,128)(4,1)} %get-tuple-element.1215) | copy-start | bytes 52 | tf_op jit(solution)/shard_map/while
  420.8 6.2 %copy-start.12 = (bf16[1,128,8,80]{1,3,2,0:T(8,128)(2,1)S(1)}, bf16[1,128,8,80]{1,3,2,0:T(8,128)(2,1)}, u32[]{:S(2)}) copy-start(bf16[1,128,8,80]{1,3,2,0:T(8,128)(2,1)} %get-tuple-element.1219) | copy-start | bytes 491524 | tf_op jit(solution)/shard_map/while
  434.7 6.0 %copy-start.17 = (pred[1,1,16]{2,1,0:T(4,128)(4,1)S(1)}, pred[1,1,16]{2,1,0:T(4,128)(4,1)}, u32[]{:S(2)}) copy-start(pred[1,1,16]{2,1,0:T(4,128)(4,1)} %get-tuple-element.1215) | copy-start | bytes 52 | tf_op jit(solution)/shard_map/while
  434.7 6.1 %copy-start.12 = (bf16[1,128,8,80]{1,3,2,0:T(8,128)(2,1)S(1)}, bf16[1,128,8,80]{1,3,2,0:T(8,128)(2,1)}, u32[]{:S(2)}) copy-start(bf16[1,128,8,80]{1,3,2,0:T(8,128)(2,1)} %get-tuple-element.1219) | copy-start | bytes 491524 | tf_op jit(solution)/shard_map/while
  447.3 19.6 %copy-start.1 = (f32[1,128,8,80]{1,3,2,0:T(8,128)S(1)}, f32[1,128,8,80]{1,3,2,0:T(8,128)}, u32[]{:S(2)}) copy-start(f32[1,128,8,80]{1,3,2,0:T(8,128)} %custom-call.4) | copy-start | bytes 983044
  546.3 12.6 %collective-permute-start = (bf16[1,1,128,1280]{3,2,1,0:T(8,128)(2,1)S(1)}, bf16[1,1,128,1280]{3,2,1,0:T(8,128)(2,1)S(1)}, u32[]{:S(2)}, u32[]{:S(2)}) collective-permute-start(bf16[1,1,128,1280]{3,2,1,0:T(8,128)(2,1)S(1)} %fusion.44), channel_id=1, source_target_pairs={{0,448},{64,0},{128,64},{192,128},{256,192},{320,256},{384,320},{4... | collective-permute-start | bytes 983048 | tf_op jit(solution)/shard_map/ppermute | solution.py:21
  (22 other events, 39.4 us)
Sparse Core Ops, SparseCore 0:
  9.5 36.7 all-gather.16
  48.4 33.9 all-gather.12
  84.5 33.9 all-gather.18
  120.5 33.9 all-gather.14
  156.4 76.3 all-gather.22
  234.7 77.3 all-gather.20
  314.2 72.2 all-gather.26
  388.6 78.1 all-gather.24
